TPU v7x, 32 devices: a whole 2x2x4 slice. The times are simulated.
32 devices in a mesh: expert: 8 (over z, x), hidden: 2 (over core), dp: 2 (over y).
Axes of the slice: x: 2, y: 2, z: 4, core: 2. Of those that a mesh axis runs over, the one named last changes fastest.
Arguments:
- inputs: bfloat16 [384, 4096], P(('expert', 'dp')), may hold values from -6 to 6
- out_grad: bfloat16 [384, 4096], P(('expert', 'dp')), may hold values from -6 to 6
- expert_ids: int32 [384, 6], P(('expert', 'dp')), may hold values from 0 to 15, all different within a row; in each aligned block of 24 rows (0 to 23, 24 to 47, ...) at most 10 rows name the same one
- gate_weights: bfloat16 [384, 6], P(('expert', 'dp')), may hold values from 0.049804688 to 0.59765625
- encode_weight: bfloat16 [4096, 1024], P(None, 'hidden'), may hold values from -0.09375 to 0.09375
- decode_weight: bfloat16 [1024, 4096], P('hidden'), may hold values from -0.1875 to 0.1875
- up_proj: bfloat16 [16, 1024, 2688], P('expert', None, 'hidden'), may hold values from -0.1875 to 0.1875
- down_proj: bfloat16 [16, 2688, 1024], P('expert', 'hidden'), may hold values from -0.125 to 0.125
Outputs:
- latent_grad: float32 [384, 1024], P(('expert', 'dp'), 'hidden')
- gate_dots: bfloat16 [384, 6], P(('expert', 'dp'))
- weight_grad: float32 [16, 2688, 1024], P('expert', 'hidden', 'dp')
Inputs may be any that keep to these rules, and one draw needn't show every extreme that they name: `expert_ids`: each row names 6 different experts; within the rows of one token group no expert is named more than 10 times, and the per-expert counts and slot offsets follow from these ids.
All inputs are finite; a program needn't handle non-finite values.
Results may differ from a plain program's by a relative error of at most 0.017.
Values may be sent and summed in bfloat16 or wider, within the bound.
A program may use at most 64 MiB of HBM per device.

v0:
```python
import functools

import jax
import jax.numpy as jnp
from jax import lax
from jax.experimental import pallas as pl
from jax.experimental.pallas import tpu as pltpu
from jax.sharding import PartitionSpec as P


def rounded(value):
    return lax.optimization_barrier(value.astype(jnp.bfloat16)).astype(jnp.float32)


def body(
    inputs, out_grad, expert_ids, gate_weights, encode_weight, decode_weight, up_proj, down_proj
):
    owners = lax.axis_size("expert")
    local_experts = up_proj.shape[0]
    experts = local_experts * owners
    tokens_here = inputs.shape[0]
    picks = expert_ids.shape[1]
    capacity = max(2, tokens_here * picks * 7 // (experts * 6))
    slots = experts * capacity
    latent_in = jnp.dot(inputs, encode_weight, preferred_element_type=jnp.float32).astype(
        jnp.bfloat16
    )
    latent_out = lax.dot_general(
        out_grad, decode_weight, (((1,), (1,)), ((), ())), preferred_element_type=jnp.float32
    ).astype(jnp.bfloat16)
    flat_ids = expert_ids.reshape(-1)
    onehot = (flat_ids[:, None] == jnp.arange(experts, dtype=jnp.int32)[None, :]).astype(jnp.int32)
    earlier = jnp.cumsum(onehot, axis=0) - onehot
    slot_index = jnp.sum(earlier * onehot, axis=1)
    target = flat_ids * capacity + slot_index
    pick_count = flat_ids.shape[0]
    owner_pick = (
        jnp.full((slots,), -1, jnp.int32).at[target].set(jnp.arange(pick_count, dtype=jnp.int32))
    )
    filled = owner_pick >= 0
    safe_pick = jnp.maximum(owner_pick, 0)
    token_of = safe_pick // picks
    send_in = jnp.where(
        filled[:, None], jnp.take(latent_in, token_of, axis=0), jnp.zeros((), jnp.bfloat16)
    )
    send_out = jnp.where(
        filled[:, None], jnp.take(latent_out, token_of, axis=0), jnp.zeros((), jnp.bfloat16)
    )
    send_gate = jnp.where(
        filled, jnp.take(gate_weights.reshape(-1), safe_pick), jnp.zeros((), jnp.bfloat16)
    )
    recv_in, recv_out, recv_gate = (
        lax.all_to_all(send_in, "expert", split_axis=0, concat_axis=0, tiled=True),
        lax.all_to_all(send_out, "expert", split_axis=0, concat_axis=0, tiled=True),
        lax.all_to_all(send_gate, "expert", split_axis=0, concat_axis=0, tiled=True),
    )
    whole_in, whole_out = (
        lax.all_gather(recv_in, "hidden", axis=1, tiled=True),
        lax.all_gather(recv_out, "hidden", axis=1, tiled=True),
    )
    latent = whole_in.shape[1]
    encoded = whole_in.reshape(owners, local_experts, capacity, latent)
    upstream = whole_out.reshape(owners, local_experts, capacity, latent)
    weight = recv_gate.astype(jnp.float32).reshape(owners, local_experts, capacity, 1)
    pre = jnp.einsum("secl,elh->sech", encoded, up_proj, preferred_element_type=jnp.float32)
    active = jnp.maximum(pre, 0.0)
    squared = (active * active).astype(jnp.bfloat16)
    proj = jnp.einsum("secl,ehl->sech", upstream, down_proj, preferred_element_type=jnp.float32)
    gate_part = (
        jnp.sum(squared.astype(jnp.float32) * proj, axis=3).astype(jnp.bfloat16).reshape(slots)
    )
    hidden_grad = (weight * proj * 2.0 * active).astype(jnp.bfloat16)
    latent_part = jnp.einsum(
        "sech,elh->secl", hidden_grad, up_proj, preferred_element_type=jnp.float32
    ).reshape(slots, latent)
    scaled = (weight * upstream.astype(jnp.float32)).astype(jnp.bfloat16)
    weight_part = jnp.einsum("sech,secl->ehl", squared, scaled, preferred_element_type=jnp.float32)
    weight_grad = lax.psum_scatter(
        rounded(weight_part).astype(jnp.bfloat16), "dp", scatter_dimension=2, tiled=True
    ).astype(jnp.float32)
    slot_grad = lax.psum_scatter(
        rounded(latent_part).astype(jnp.bfloat16), "hidden", scatter_dimension=1, tiled=True
    ).astype(jnp.float32)
    back_grad, back_gate = (
        lax.all_to_all(
            slot_grad.astype(jnp.bfloat16), "expert", split_axis=0, concat_axis=0, tiled=True
        ).astype(slot_grad.dtype),
        lax.all_to_all(
            gate_part.astype(jnp.float32).astype(jnp.bfloat16),
            "expert",
            split_axis=0,
            concat_axis=0,
            tiled=True,
        ).astype(jnp.float32),
    )
    pick_grad = jnp.take(back_grad, target, axis=0)
    latent_grad = jnp.sum(pick_grad.reshape(tokens_here, picks, -1), axis=1)
    gate_local = jnp.take(back_gate, target).reshape(tokens_here, picks)
    gate_dots = lax.psum(gate_local, "hidden").astype(jnp.bfloat16)
    return (latent_grad, gate_dots, weight_grad)


LANES = 128
MESH = pl.DeviceIdType.MESH
(
    UP_S, DOWN_S, SIDE_S, DX_R, UY_S, DOWNY_S, SIDEY_S, DY_R, FX_S, FX_R, FY_S, FY_R,
    YX_S, YX_R, YY_S, YY_R, GX_S, GX_R, GY_S, GY_R, PS_S, PS_R, TS_S, TS_R,
) = range(24)
NT = (((1,), (1,)), ((), ()))
TN = (((0,), (0,)), ((), ()))


def dot(a, b, dims):
    return lax.dot_general(a, b, dims, preferred_element_type=jnp.float32)


def pad_rows(value, rows):
    extra = rows - value.shape[0]
    if extra == 0:
        return value
    return jnp.concatenate([value, jnp.zeros((extra, value.shape[1]), value.dtype)], axis=0)


def kernel(
    owners, chunks, steps,
    ids_ref, gate_ref, x_hbm, g_hbm, enc_hbm, dec_hbm, up_hbm, down_hbm,
    fin_ref, sq_hbm, sc_hbm,
    x_v, g_v, enc, dec, up, down, xg, yb, hgt, wt, gt, tr, lgo, ps, pr, ts, trb, sq_ref, sc_ref,
    sem, loc,
):
    me, h, d = lax.axis_index("expert"), lax.axis_index("hidden"), lax.axis_index("dp")
    local, units = up.shape[0], up.shape[1]
    half = enc.shape[1]
    picks, tokens = ids_ref.shape
    block = xg.shape[3]
    rows = owners * block
    piece = units // chunks
    other = {"hidden": 1 - h}
    across = {"dp": 1 - d}

    depth = enc.shape[0] // steps
    width = dec.shape[0] // steps
    copies = [pltpu.make_async_copy(x_hbm, x_v, loc.at[0])]
    for i in range(steps):
        part = pl.ds(i * depth, depth)
        copies.append(pltpu.make_async_copy(enc_hbm.at[part], enc.at[part], loc.at[1 + i]))
    copies.append(pltpu.make_async_copy(g_hbm, g_v, loc.at[1 + steps]))
    for i in range(steps):
        part = pl.ds(i * width, width)
        copies.append(pltpu.make_async_copy(dec_hbm.at[part], dec.at[part], loc.at[2 + steps + i]))
    copies.append(pltpu.make_async_copy(up_hbm, up, loc.at[2 + 2 * steps]))
    copies.append(pltpu.make_async_copy(down_hbm, down, loc.at[3 + 2 * steps]))
    for copy in copies[: 2 + 2 * steps]:
        copy.start()

    live = pl.ds(0, tokens)
    spare = block - 16
    if tokens < block:
        xg[:, :, :, spare:block, :] = jnp.zeros((2, 2, owners, 16, half + LANES), jnp.bfloat16)
        yb[:, :, :, spare:block, :] = jnp.zeros((2, 2, owners, 16, half), jnp.bfloat16)

    barrier = pltpu.get_barrier_semaphore()
    for j in range(1, owners):
        pl.semaphore_signal(barrier, inc=1, device_id={"expert": lax.rem(me + j, owners)}, device_id_type=MESH)
    pl.semaphore_signal(barrier, inc=1, device_id=other, device_id_type=MESH)
    pl.semaphore_signal(barrier, inc=1, device_id=across, device_id_type=MESH)


    def remote(src, dst, s_kind, s_at, r_kind, r_at, device):
        return pltpu.make_async_remote_copy(
            src_ref=src, dst_ref=dst, send_sem=sem.at[s_kind, s_at], recv_sem=sem.at[r_kind, r_at],
            device_id=device, device_id_type=MESH,
        )

    side = lax.rem(me, 2)
    level, levels = me // 2, owners // 2
    aside = {"expert": me + 1 - 2 * side}
    above = {"expert": lax.rem(me + 2, owners)}
    below = {"expert": lax.rem(me + owners - 2, owners)}

    def x_same(at, s_kind, device):
        part = xg.at[0, h, at, live]
        return remote(part, part, s_kind, at, DX_R, at, device)

    def y_same(at, s_kind, device):
        part = yb.at[0, h, at, live]
        return remote(part, part, s_kind, at, DY_R, at, device)

    def x_pass(at):
        part = xg.at[0, h, at, live]
        return remote(part, part, FX_S, at, FX_R, at, other)

    def y_pass(at):
        part = yb.at[0, h, at, live]
        return remote(part, part, FY_S, at, FY_R, at, other)

    def x_across(at):
        return remote(xg.at[0, h, at, live], xg.at[1, h, at, live], YX_S, at, YX_R, at, across)

    def y_across(at):
        return remote(yb.at[0, h, at, live], yb.at[1, h, at, live], YY_S, at, YY_R, at, across)

    def x_far(at):
        part = xg.at[1, h, at, live]
        return remote(part, part, GX_S, at, GX_R, at, other)

    def y_far(at):
        part = yb.at[1, h, at, live]
        return remote(part, part, GY_S, at, GY_R, at, other)

    def x_near(at):
        x_pass(at).start()
        x_across(at).start()

    def y_near(at):
        y_pass(at).start()

        @pl.when(h == 1 - d)
        def _():
            y_across(at).start()

    def climb(at, move):
        @pl.when(level < levels - 1)
        def _():
            (x_same(at, UP_S, above) if move == "x" else y_same(at, UY_S, above)).start()

    def descend(at, move):
        @pl.when(level > 0)
        def _():
            (x_same(at, DOWN_S, below) if move == "x" else y_same(at, DOWNY_S, below)).start()

    def sideways(at, move):
        (x_same(at, SIDE_S, aside) if move == "x" else y_same(at, SIDEY_S, aside)).start()

    def arrived(at, move):
        (x_same(at, SIDE_S, aside) if move == "x" else y_same(at, SIDEY_S, aside)).wait_recv()

    expert_rows = lax.broadcasted_iota(jnp.int32, (LANES, tokens), 0)
    spread = jnp.zeros((LANES, tokens), jnp.float32)
    for k in range(picks):
        spread += jnp.where(
            ids_ref[k : k + 1, :] == expert_rows, gate_ref[k : k + 1, :].astype(jnp.float32), 0.0
        )
    tr[...] = jnp.zeros_like(tr)
    tr[:, 0:tokens] = spread
    own_gates = tr[...].T[0:block, :].astype(jnp.bfloat16)
    gt[...] = jnp.zeros_like(gt)

    copies[0].wait()
    total = jnp.zeros((tokens, half), jnp.float32)
    for i in range(steps):
        copies[1 + i].wait()
        total += jnp.dot(
            x_v[:, i * depth : (i + 1) * depth], enc[i * depth : (i + 1) * depth, :],
            preferred_element_type=jnp.float32,
        )
    xg[0, h, me, :, 0:half] = pad_rows(total, block).astype(jnp.bfloat16)
    xg[0, h, me, :, half : half + LANES] = own_gates
    copies[2 + 2 * steps].start()
    copies[3 + 2 * steps].start()
    pl.semaphore_wait(barrier, owners + 1)

    climb(me, "x")
    descend(me, "x")
    sideways(me, "x")
    x_near(me)

    copies[1 + steps].wait()
    for i in range(steps):
        copies[2 + steps + i].wait()
    for i in range(steps):
        got = dot(g_v[...], dec[i * width : (i + 1) * width, :], NT)
        yb[0, h, me, :, i * width : (i + 1) * width] = pad_rows(got, block).astype(jnp.bfloat16)

    climb(me, "y")
    descend(me, "y")
    sideways(me, "y")
    y_near(me)

    def relay(far, move):
        near = x_near if move == "x" else y_near

        @pl.when(level >= far)
        def _():
            at = me - 2 * far
            arrived(at, move)
            climb(at, move)
            sideways(at, move)
            near(at)

        @pl.when(level + far < levels)
        def _():
            at = me + 2 * far
            arrived(at, move)
            descend(at, move)
            sideways(at, move)
            near(at)

    def collect(far, move):
        near = x_near if move == "x" else y_near
        twin = me + 1 - 2 * side

        @pl.when(level >= far)
        def _():
            arrived(twin - 2 * far, move)
            near(twin - 2 * far)

        if far > 0:

            @pl.when(level + far < levels)
            def _():
                arrived(twin + 2 * far, move)
                near(twin + 2 * far)

    for far in range(1, levels):
        relay(far, "x")
        collect(far - 1, "x")
        relay(far, "y")
        collect(far - 1, "y")
    collect(levels - 1, "x")
    collect(levels - 1, "y")

    copies[2 + 2 * steps].wait()
    copies[3 + 2 * steps].wait()

    @pl.loop(0, owners)
    def _(s):
        remote(xg.at[0, 1 - h, s, live], xg.at[0, 1 - h, s, live], FX_S, s, FX_R, s, other).wait_recv()
        remote(yb.at[0, 1 - h, s, live], yb.at[0, 1 - h, s, live], FY_S, s, FY_R, s, other).wait_recv()

    def gates_of(side):
        return xg[side, h, :, :, half : half + LANES].reshape(rows, LANES).astype(jnp.float32)

    wt[...] = gates_of(0).T

    def pre_of(side, e, span):
        return dot(up[e, span, 0:half], xg[side, 0, :, :, 0:half].reshape(rows, half), NT) + dot(
            up[e, span, half : 2 * half], xg[side, 1, :, :, 0:half].reshape(rows, half), NT
        )

    @pl.loop(0, local * chunks)
    def _(step):
        e = step // chunks
        c = step % chunks
        span = pl.ds(pl.multiple_of(c * piece, piece), piece)
        active = jnp.maximum(pre_of(0, e, span), 0.0)
        squared = (active * active).astype(jnp.bfloat16)
        sq_ref[0, e, span, :] = squared
        proj = dot(down[e, span, 0:half], yb[0, 0].reshape(rows, half), NT) + dot(
            down[e, span, half : 2 * half], yb[0, 1].reshape(rows, half), NT
        )
        at = pl.ds(me * local + e, 1)
        gt[at, :] += jnp.sum(squared.astype(jnp.float32) * proj, axis=0, keepdims=True)
        grad = wt[at, :] * proj * 2.0 * active
        hgt[e, span, :] = grad.astype(jnp.bfloat16)

    out_own = pltpu.make_async_copy(sq_ref.at[0], sq_hbm.at[0], loc.at[4 + 2 * steps])
    out_own.start()

    @pl.loop(0, owners)
    def _(s):
        remote(xg.at[1, h, s, live], xg.at[1, h, s, live], YX_S, s, YX_R, s, across).wait_recv()
        x_far(s).start()

        @pl.when(h == d)
        def _():
            remote(yb.at[1, h, s, live], yb.at[1, h, s, live], YY_S, s, YY_R, s, across).wait_recv()
            y_far(s).start()

    tile = 2 * LANES if half % (2 * LANES) == 0 else LANES

    def latent_tile(which, t):
        column = pl.ds(pl.multiple_of(which * half + t * tile, tile), tile)
        out = dot(hgt[0], up[0, :, column], TN)
        for e in range(1, local):
            out += dot(hgt[e], up[e, :, column], TN)
        return out

    gate_cols = gt[...].T.astype(jnp.bfloat16)
    ps[:, :, half : half + LANES] = gate_cols.reshape(owners, block, LANES)

    @pl.loop(0, half // tile)
    def _(t):
        span = pl.ds(pl.multiple_of(t * tile, tile), tile)
        ps[:, :, span] = latent_tile(1 - h, t).astype(jnp.bfloat16).reshape(owners, block, tile)

    swap = remote(ps, pr, PS_S, 0, PS_R, 0, other)
    swap.start()

    @pl.loop(0, half // tile)
    def _(t):
        span = pl.ds(pl.multiple_of(t * tile, tile), tile)
        lgo[:, span] = latent_tile(h, t)

    swap.wait_recv()
    ts[:, :, 0:half] = (
        (lgo[...] + pr[:, :, 0:half].reshape(rows, half).astype(jnp.float32))
        .astype(jnp.bfloat16)
        .reshape(owners, block, half)
    )
    ts[:, :, half : half + LANES] = (
        (gate_cols.astype(jnp.float32) + pr[:, :, half : half + LANES].reshape(rows, LANES).astype(jnp.float32))
        .astype(jnp.bfloat16)
        .reshape(owners, block, LANES)
    )

    def give(at, s_at, r_at):
        return remote(ts.at[at, live], trb.at[r_at, live], TS_S, s_at, TS_R, r_at, {"expert": at})

    @pl.loop(1, owners)
    def _(j):
        peer = lax.rem(me + j, owners)
        give(peer, peer, me).start()

    trb[me] = ts[me]

    @pl.loop(0, owners)
    def _(s):
        remote(xg.at[1, 1 - h, s, live], xg.at[1, 1 - h, s, live], GX_S, s, GX_R, s, other).wait_recv()

        @pl.when(h == 1 - d)
        def _():
            remote(yb.at[1, 1 - h, s, live], yb.at[1, 1 - h, s, live], GY_S, s, GY_R, s, other).wait_recv()

    @pl.loop(0, local * chunks)
    def _(step):
        e = step // chunks
        c = step % chunks
        span = pl.ds(pl.multiple_of(c * piece, piece), piece)
        active = jnp.maximum(pre_of(1, e, span), 0.0)
        sq_ref[1, e, span, :] = (active * active).astype(jnp.bfloat16)

    out_other = pltpu.make_async_copy(sq_ref.at[1], sq_hbm.at[1], loc.at[5 + 2 * steps])
    out_other.start()
    lane = lax.broadcasted_iota(jnp.int32, (rows, LANES), 1)
    for part in range(2):
        gates = gates_of(part)
        mine = yb[part, d].reshape(rows, half).astype(jnp.float32)
        for e in range(local):
            column = jnp.sum(jnp.where(lane == me * local + e, gates, 0.0), axis=1, keepdims=True)
            sc_ref[part, e] = (column * mine).astype(jnp.bfloat16)

    out_scaled = pltpu.make_async_copy(sc_ref, sc_hbm, loc.at[6 + 2 * steps])
    out_scaled.start()

    @pl.loop(1, owners)
    def _(j):
        s = lax.rem(me - j + owners, owners)
        give(s, s, s).wait_recv()

    final = trb[0].astype(jnp.float32)
    for s in range(1, owners):
        final += trb[s].astype(jnp.float32)
    fin_ref[...] = final
    out_own.wait()
    out_other.wait()
    out_scaled.wait()
    swap.wait_send()

    @pl.loop(1, owners)
    def _(j):
        s = lax.rem(me + j, owners)
        give(s, s, s).wait_send()

    @pl.loop(0, owners)
    def _(s):
        x_pass(s).wait_send()
        y_pass(s).wait_send()
        x_across(s).wait_send()
        x_far(s).wait_send()

        @pl.when(h == 1 - d)
        def _():
            y_across(s).wait_send()

        @pl.when(h == d)
        def _():
            y_far(s).wait_send()

    @pl.loop(0, levels)
    def _(z):
        at = 2 * z + side
        x_same(at, SIDE_S, aside).wait_send()
        y_same(at, SIDEY_S, aside).wait_send()

        @pl.when((z <= level) & (level < levels - 1))
        def _():
            x_same(at, UP_S, above).wait_send()
            y_same(at, UY_S, above).wait_send()

        @pl.when((z >= level) & (level > 0))
        def _():
            x_same(at, DOWN_S, below).wait_send()
            y_same(at, DOWNY_S, below).wait_send()


def finish(ids_ref, fin_ref, sq_ref, sc_ref, lat_ref, dots_ref, grad_ref, tr, row):
    picks, tokens = ids_ref.shape
    half = lat_ref.shape[1]

    @pl.when((pl.program_id(0) == 0) & (pl.program_id(1) == 0))
    def _():
        lat_ref[...] = fin_ref[0:tokens, 0:half]
        tr[...] = jnp.zeros_like(tr)
        tr[0 : fin_ref.shape[0], :] = fin_ref[:, half : half + LANES]
        turned = tr[...].T[:, 0:tokens]
        expert_rows = lax.broadcasted_iota(jnp.int32, (LANES, tokens), 0)
        for k in range(picks):
            row[k : k + 1, 0:tokens] = jnp.sum(
                jnp.where(ids_ref[k : k + 1, :] == expert_rows, turned, 0.0), axis=0, keepdims=True
            )
        dots_ref[...] = row[0:picks, 0:tokens].astype(jnp.bfloat16)

    grad_ref[0] = jnp.dot(
        sq_ref[0, 0], sc_ref[0, 0], preferred_element_type=jnp.float32
    ) + jnp.dot(sq_ref[1, 0], sc_ref[1, 0], preferred_element_type=jnp.float32)


def dense_body(
    inputs, out_grad, expert_ids, gate_weights, encode_weight, decode_weight, up_proj, down_proj
):
    owners = lax.axis_size("expert")
    tokens, width = inputs.shape
    picks = expert_ids.shape[1]
    local, latent, units = up_proj.shape
    half = encode_weight.shape[1]
    block = -(-tokens // 16) * 16
    rows = owners * block
    chunks = 2 if units % 32 == 0 else 1
    steps = 4
    bf16, f32 = jnp.bfloat16, jnp.float32
    up_t = jnp.swapaxes(up_proj, 1, 2)
    vmem, hbm = pl.BlockSpec(memory_space=pltpu.VMEM), pl.BlockSpec(memory_space=pl.ANY)
    fin, squared, scaled = pl.pallas_call(
        functools.partial(kernel, owners, chunks, steps),
        out_shape=(
            jax.ShapeDtypeStruct((block, half + LANES), f32),
            jax.ShapeDtypeStruct((2, local, units, rows), bf16),
            jax.ShapeDtypeStruct((2, local, rows, half), bf16),
        ),
        in_specs=[vmem, vmem] + [hbm] * 6,
        out_specs=(vmem, hbm, hbm),
        scratch_shapes=[
            pltpu.VMEM((tokens, width), bf16),
            pltpu.VMEM((tokens, width), bf16),
            pltpu.VMEM((width, half), bf16),
            pltpu.VMEM((half, width), bf16),
            pltpu.VMEM((local, units, latent), bf16),
            pltpu.VMEM((local, units, latent), bf16),
            pltpu.VMEM((2, 2, owners, block, half + LANES), bf16),
            pltpu.VMEM((2, 2, owners, block, half), bf16),
            pltpu.VMEM((local, units, rows), bf16),
            pltpu.VMEM((LANES, rows), f32),
            pltpu.VMEM((LANES, rows), f32),
            pltpu.VMEM((LANES, LANES), f32),
            pltpu.VMEM((rows, half), f32),
            pltpu.VMEM((owners, block, half + LANES), bf16),
            pltpu.VMEM((owners, block, half + LANES), bf16),
            pltpu.VMEM((owners, block, half + LANES), bf16),
            pltpu.VMEM((owners, block, half + LANES), bf16),
            pltpu.VMEM((2, local, units, rows), bf16),
            pltpu.VMEM((2, local, rows, half), bf16),
            pltpu.SemaphoreType.DMA((24, owners)),
            pltpu.SemaphoreType.DMA((7 + 2 * steps,)),
        ],
        compiler_params=pltpu.CompilerParams(
            collective_id=0, has_side_effects=True, vmem_limit_bytes=60 * 2**20
        ),
    )(expert_ids.T, gate_weights.T, inputs, out_grad, encode_weight, decode_weight, up_t, down_proj)
    cuts = 2 if units % 32 == 0 else 1
    piece = units // cuts
    lat, dots, weight_grad = pl.pallas_call(
        finish,
        grid=(local, cuts),
        out_shape=(
            jax.ShapeDtypeStruct((tokens, half), f32),
            jax.ShapeDtypeStruct((picks, tokens), bf16),
            jax.ShapeDtypeStruct((local, units, half), f32),
        ),
        in_specs=[
            pl.BlockSpec((picks, tokens), lambda e, c: (0, 0)),
            pl.BlockSpec((block, half + LANES), lambda e, c: (0, 0)),
            pl.BlockSpec((2, 1, piece, rows), lambda e, c: (0, e, c, 0)),
            pl.BlockSpec((2, 1, rows, half), lambda e, c: (0, e, 0, 0)),
        ],
        out_specs=(
            pl.BlockSpec((tokens, half), lambda e, c: (0, 0)),
            pl.BlockSpec((picks, tokens), lambda e, c: (0, 0)),
            pl.BlockSpec((1, piece, half), lambda e, c: (e, c, 0)),
        ),
        scratch_shapes=[pltpu.VMEM((LANES, LANES), f32), pltpu.VMEM((8, LANES), f32)],
    )(expert_ids.T, fin, squared, scaled)
    return lat, dots.T, weight_grad


def pick_body(mesh):
    shape = mesh.shape
    fits = shape["hidden"] == 2 and shape["dp"] == 2 and shape["expert"] % 2 == 0
    return dense_body if fits else body


def solution(mesh):
    return jax.shard_map(
        pick_body(mesh),
        mesh=mesh,
        in_specs=(
            P(("expert", "dp"), None),
            P(("expert", "dp"), None),
            P(("expert", "dp"), None),
            P(("expert", "dp"), None),
            P(None, "hidden"),
            P("hidden", None),
            P("expert", None, "hidden"),
            P("expert", "hidden", None),
        ),
        out_specs=(
            P(("expert", "dp"), "hidden"),
            P(("expert", "dp"), None),
            P("expert", "hidden", "dp"),
        ),
        check_vma=False,
    )
```

profile of v0, /device:TPU:0, one launch (start us, length us, event | category | flops | bytes accessed | tf_op | source)
XLA Modules:
  0.0 42.7 jit_solution(11994509861349089895)
XLA Ops:
  0.6 35.7 %shard_map.103 = (f32[32,640]{1,0:T(8,128)}, bf16[2,2,1344,256]{3,2,1,0:T(8,128)(2,1)}, bf16[2,2,256,512]{3,2,1,0:T(8,128)(2,1)}) custom-call(s32[6,24]{1,0:T(8,128)} %bitcast.5, bf16[6,24]{1,0:T(8,128)(2,1)} %bitcast.7, bf16[24,4096]{1,0:T(8,128)(2,1)} %x_hbm.1, bf16[24,4096]{1,0:T(8,128)(2,1)} %g_hbm.1, bf16[4096,512]{1,0:T(8,128)(2,1)} %enc_hbm.1, ...), custom_call_target="tpu_custom_call" | custom-call | tf_op jit(solution)/shard_map/pallas_call | solution.py:534
  36.4 6.3 %shard_map.104 = (f32[24,512]{1,0:T(8,128)}, bf16[6,24]{1,0:T(8,128)(2,1)}, f32[2,1344,512]{2,1,0:T(8,128)}) custom-call(s32[6,24]{1,0:T(8,128)} %bitcast.6, f32[32,640]{1,0:T(8,128)} %get-tuple-element.9.fin_ref, bf16[2,2,1344,256]{3,2,1,0:T(8,128)(2,1)} %get-tuple-element.10.sq_ref, bf16[2,2,256,512]{3,2,1,0:T(8,128)(2,1)} %get-tuple-element.11.sc_ref), custom_call_target="tpu_custom_call" | custom-call | tf_op jit(solution)/shard_map/pallas_call | solution.py:572
where the time goes:
time: 42.9 us; the launch traced here: 42.7 us
  Pallas kernels  42.1 us (98%)
  between operations  0.64 us (1%)
    pallas_call x1, Pallas kernels, dense_body(): pl.pallas_call(functools.partial(kernel, owners, chunks, steps), out_shap...  35.7 us
    pallas_call x1, Pallas kernels, dense_body(): pl.pallas_call(finish, grid=(local, cuts), out_shape=(jax.ShapeDtypeStruc...  6.33 us

commit v1 on v0

--- a/solution.py
+++ b/solution.py
@@ -123,9 +123,9 @@
 
 def kernel(
     owners, chunks, steps,
-    ids_ref, gate_ref, x_hbm, g_hbm, enc_hbm, dec_hbm, up_hbm, down_hbm,
-    fin_ref, sq_hbm, sc_hbm,
-    x_v, g_v, enc, dec, up, down, xg, yb, hgt, wt, gt, tr, lgo, ps, pr, ts, trb, sq_ref, sc_ref,
+    ids_hbm, gate_hbm, x_hbm, g_hbm, enc_hbm, dec_hbm, up_hbm, down_hbm,
+    lat_ref, dots_ref, wg_ref,
+    ids_ref, gate_ref, x_v, g_v, enc, dec, up, down, xg, yb, hgt, wt, gt, tr, lgo, ps, pr, ts, trb, sq_ref, sc_ref,
     sem, loc,
 ):
     me, h, d = lax.axis_index("expert"), lax.axis_index("hidden"), lax.axis_index("dp")
@@ -150,7 +150,11 @@
         copies.append(pltpu.make_async_copy(dec_hbm.at[part], dec.at[part], loc.at[2 + steps + i]))
     copies.append(pltpu.make_async_copy(up_hbm, up, loc.at[2 + 2 * steps]))
     copies.append(pltpu.make_async_copy(down_hbm, down, loc.at[3 + 2 * steps]))
-    for copy in copies[: 2 + 2 * steps]:
+    small = [
+        pltpu.make_async_copy(ids_hbm, ids_ref, loc.at[4 + 2 * steps]),
+        pltpu.make_async_copy(gate_hbm, gate_ref, loc.at[5 + 2 * steps]),
+    ]
+    for copy in small + copies[: 2 + 2 * steps]:
         copy.start()
 
     live = pl.ds(0, tokens)
@@ -235,6 +239,8 @@
     def arrived(at, move):
         (x_same(at, SIDE_S, aside) if move == "x" else y_same(at, SIDEY_S, aside)).wait_recv()
 
+    small[0].wait()
+    small[1].wait()
     expert_rows = lax.broadcasted_iota(jnp.int32, (LANES, tokens), 0)
     spread = jnp.zeros((LANES, tokens), jnp.float32)
     for k in range(picks):
@@ -354,9 +360,6 @@
         grad = wt[at, :] * proj * 2.0 * active
         hgt[e, span, :] = grad.astype(jnp.bfloat16)
 
-    out_own = pltpu.make_async_copy(sq_ref.at[0], sq_hbm.at[0], loc.at[4 + 2 * steps])
-    out_own.start()
-
     @pl.loop(0, owners)
     def _(s):
         remote(xg.at[1, h, s, live], xg.at[1, h, s, live], YX_S, s, YX_R, s, across).wait_recv()
@@ -430,8 +433,6 @@
         active = jnp.maximum(pre_of(1, e, span), 0.0)
         sq_ref[1, e, span, :] = (active * active).astype(jnp.bfloat16)
 
-    out_other = pltpu.make_async_copy(sq_ref.at[1], sq_hbm.at[1], loc.at[5 + 2 * steps])
-    out_other.start()
     lane = lax.broadcasted_iota(jnp.int32, (rows, LANES), 1)
     for part in range(2):
         gates = gates_of(part)
@@ -440,8 +441,14 @@
             column = jnp.sum(jnp.where(lane == me * local + e, gates, 0.0), axis=1, keepdims=True)
             sc_ref[part, e] = (column * mine).astype(jnp.bfloat16)
 
-    out_scaled = pltpu.make_async_copy(sc_ref, sc_hbm, loc.at[6 + 2 * steps])
-    out_scaled.start()
+    @pl.loop(0, local * chunks)
+    def _(step):
+        e = step // chunks
+        c = step % chunks
+        span = pl.ds(pl.multiple_of(c * piece, piece), piece)
+        wg_ref[e, span, :] = jnp.dot(
+            sq_ref[0, e, span, :], sc_ref[0, e], preferred_element_type=jnp.float32
+        ) + jnp.dot(sq_ref[1, e, span, :], sc_ref[1, e], preferred_element_type=jnp.float32)
 
     @pl.loop(1, owners)
     def _(j):
@@ -451,10 +458,15 @@
     final = trb[0].astype(jnp.float32)
     for s in range(1, owners):
         final += trb[s].astype(jnp.float32)
-    fin_ref[...] = final
-    out_own.wait()
-    out_other.wait()
-    out_scaled.wait()
+    lat_ref[...] = final[0:tokens, 0:half]
+    tr[...] = jnp.zeros_like(tr)
+    tr[0:block, :] = final[:, half : half + LANES]
+    turned = tr[...].T[:, 0:tokens]
+    picked = [
+        jnp.sum(jnp.where(ids_ref[k : k + 1, :] == expert_rows, turned, 0.0), axis=0, keepdims=True)
+        for k in range(picks)
+    ]
+    dots_ref[...] = jnp.concatenate(picked, axis=0).astype(jnp.bfloat16)
     swap.wait_send()
 
     @pl.loop(1, owners)
@@ -494,26 +506,16 @@
             y_same(at, DOWNY_S, below).wait_send()
 
 
-def finish(ids_ref, fin_ref, sq_ref, sc_ref, lat_ref, dots_ref, grad_ref, tr, row):
-    picks, tokens = ids_ref.shape
-    half = lat_ref.shape[1]
-
-    @pl.when((pl.program_id(0) == 0) & (pl.program_id(1) == 0))
-    def _():
-        lat_ref[...] = fin_ref[0:tokens, 0:half]
-        tr[...] = jnp.zeros_like(tr)
-        tr[0 : fin_ref.shape[0], :] = fin_ref[:, half : half + LANES]
-        turned = tr[...].T[:, 0:tokens]
-        expert_rows = lax.broadcasted_iota(jnp.int32, (LANES, tokens), 0)
-        for k in range(picks):
-            row[k : k + 1, 0:tokens] = jnp.sum(
-                jnp.where(ids_ref[k : k + 1, :] == expert_rows, turned, 0.0), axis=0, keepdims=True
-            )
-        dots_ref[...] = row[0:picks, 0:tokens].astype(jnp.bfloat16)
-
-    grad_ref[0] = jnp.dot(
-        sq_ref[0, 0], sc_ref[0, 0], preferred_element_type=jnp.float32
-    ) + jnp.dot(sq_ref[1, 0], sc_ref[1, 0], preferred_element_type=jnp.float32)
+def finish(lat_vmem, dots_vmem, wg_vmem, lat_ref, dots_ref, grad_ref, loc):
+    moves = [
+        pltpu.make_async_copy(wg_vmem, grad_ref, loc.at[0]),
+        pltpu.make_async_copy(lat_vmem, lat_ref, loc.at[1]),
+        pltpu.make_async_copy(dots_vmem, dots_ref, loc.at[2]),
+    ]
+    for move in moves:
+        move.start()
+    for move in moves:
+        move.wait()
 
 
 def dense_body(
@@ -530,17 +532,23 @@
     steps = 4
     bf16, f32 = jnp.bfloat16, jnp.float32
     up_t = jnp.swapaxes(up_proj, 1, 2)
-    vmem, hbm = pl.BlockSpec(memory_space=pltpu.VMEM), pl.BlockSpec(memory_space=pl.ANY)
-    fin, squared, scaled = pl.pallas_call(
+    vmem, hbm = pl.BlockSpec(memory_space=pltpu.VMEM), pl.BlockSpec(memory_space=pltpu.HBM)
+    staged = [
+        pltpu.with_memory_space_constraint(array, pltpu.HBM)
+        for array in (expert_ids.T, gate_weights.T, inputs, out_grad, encode_weight, decode_weight, up_t, down_proj)
+    ]
+    parts = pl.pallas_call(
         functools.partial(kernel, owners, chunks, steps),
         out_shape=(
-            jax.ShapeDtypeStruct((block, half + LANES), f32),
-            jax.ShapeDtypeStruct((2, local, units, rows), bf16),
-            jax.ShapeDtypeStruct((2, local, rows, half), bf16),
+            pltpu.VMEM((tokens, half), f32),
+            pltpu.VMEM((picks, tokens), bf16),
+            pltpu.VMEM((local, units, half), f32),
         ),
-        in_specs=[vmem, vmem] + [hbm] * 6,
-        out_specs=(vmem, hbm, hbm),
+        in_specs=[hbm] * 8,
+        out_specs=(vmem, vmem, vmem),
         scratch_shapes=[
+            pltpu.VMEM((picks, tokens), jnp.int32),
+            pltpu.VMEM((picks, tokens), bf16),
             pltpu.VMEM((tokens, width), bf16),
             pltpu.VMEM((tokens, width), bf16),
             pltpu.VMEM((width, half), bf16),
@@ -564,32 +572,21 @@
             pltpu.SemaphoreType.DMA((7 + 2 * steps,)),
         ],
         compiler_params=pltpu.CompilerParams(
-            collective_id=0, has_side_effects=True, vmem_limit_bytes=60 * 2**20
+            collective_id=0, has_side_effects=True, vmem_limit_bytes=48 * 2**20
         ),
-    )(expert_ids.T, gate_weights.T, inputs, out_grad, encode_weight, decode_weight, up_t, down_proj)
-    cuts = 2 if units % 32 == 0 else 1
-    piece = units // cuts
+    )(*staged)
     lat, dots, weight_grad = pl.pallas_call(
         finish,
-        grid=(local, cuts),
         out_shape=(
             jax.ShapeDtypeStruct((tokens, half), f32),
             jax.ShapeDtypeStruct((picks, tokens), bf16),
             jax.ShapeDtypeStruct((local, units, half), f32),
         ),
-        in_specs=[
-            pl.BlockSpec((picks, tokens), lambda e, c: (0, 0)),
-            pl.BlockSpec((block, half + LANES), lambda e, c: (0, 0)),
-            pl.BlockSpec((2, 1, piece, rows), lambda e, c: (0, e, c, 0)),
-            pl.BlockSpec((2, 1, rows, half), lambda e, c: (0, e, 0, 0)),
-        ],
-        out_specs=(
-            pl.BlockSpec((tokens, half), lambda e, c: (0, 0)),
-            pl.BlockSpec((picks, tokens), lambda e, c: (0, 0)),
-            pl.BlockSpec((1, piece, half), lambda e, c: (e, c, 0)),
-        ),
-        scratch_shapes=[pltpu.VMEM((LANES, LANES), f32), pltpu.VMEM((8, LANES), f32)],
-    )(expert_ids.T, fin, squared, scaled)
+        in_specs=[vmem] * 3,
+        out_specs=(hbm, hbm, hbm),
+        scratch_shapes=[pltpu.SemaphoreType.DMA((3,))],
+        compiler_params=pltpu.CompilerParams(vmem_limit_bytes=2**20),
+    )(*parts)
     return lat, dots.T, weight_grad
 
 

time: 42.9 us -> 38.4 us (0.90)
  Pallas kernels: 42.1 us -> 37.6 us
    pallas_call x1, Pallas kernels: 6.33 us -> 2.48 us  [dense_body(): pl.pallas_call(finish, out_shape=(jax.ShapeDtypeStruct((tokens, half), f3...]
    pallas_call x1, Pallas kernels: 35.7 us -> 35.1 us  [dense_body(): pl.pallas_call(functools.partial(kernel, owners, chunks, steps), out_shap...]
where the time goes in v1:
time: 38.4 us; the launch traced here: 38.2 us
  Pallas kernels  37.6 us (98%)
  between operations  0.64 us (2%)
    pallas_call x1, Pallas kernels, dense_body(): pl.pallas_call(functools.partial(kernel, owners, chunks, steps), out_shap...  35.1 us
    pallas_call x1, Pallas kernels, dense_body(): pl.pallas_call(finish, out_shape=(jax.ShapeDtypeStruct((tokens, half), f3...  2.48 us

profile of v1, /device:TPU:0, one launch (start us, length us, event | category | flops | bytes accessed | tf_op | source)
XLA Modules:
  0.0 38.2 jit_solution(15378080359198345213)
XLA Ops:
  0.6 35.1 %shard_map.103 = (f32[24,512]{1,0:T(8,128)S(1)}, bf16[6,24]{1,0:T(8,128)(2,1)S(1)}, f32[2,1344,512]{2,1,0:T(8,128)S(1)}) custom-call(s32[6,24]{1,0:T(8,128)} %bitcast.5, bf16[6,24]{1,0:T(8,128)(2,1)} %bitcast.6, bf16[24,4096]{1,0:T(8,128)(2,1)} %x_hbm.1, bf16[24,4096]{1,0:T(8,128)(2,1)} %g_hbm.1, bf16[4096,512]{1,0:T(8,128)(2,1)} %enc_hbm.1, ...), custom_call_target="tpu_custom_call" | custom-call | tf_op jit(solution)/shard_map/pallas_call | solution.py:540
  35.8 2.5 %shard_map.104 = (f32[24,512]{1,0:T(8,128)}, bf16[6,24]{1,0:T(8,128)(2,1)}, f32[2,1344,512]{2,1,0:T(8,128)}) custom-call(f32[24,512]{1,0:T(8,128)S(1)} %get-tuple-element.9.lat_vmem, bf16[6,24]{1,0:T(8,128)(2,1)S(1)} %get-tuple-element.10.dots_vmem, f32[2,1344,512]{2,1,0:T(8,128)S(1)} %get-tuple-element.11.wg_vmem), custom_call_target="tpu_custom_call" | custom-call | tf_op jit(solution)/shard_map/pallas_call | solution.py:578
